TPU v7x, 32 devices: a whole 2x2x4 slice. The times are simulated.
32 devices in a mesh: groups: 2 (over y), seq: 4 (over z), head: 4 (over x, core).
Axes of the slice: x: 2, y: 2, z: 4, core: 2. Of those that a mesh axis runs over, the one named last changes fastest.
Arguments:
- query_latent_rows: bfloat16 [640, 1536], P(('groups', 'seq')), parts along dimension 0, may hold values from -6 to 6
- key_value_latents: bfloat16 [640, 576], P(('groups', 'seq')), parts along dimension 0, may hold values from -500 to 500
- positions: int32 [640], P(('groups', 'seq')), parts along dimension 0, may hold values from 130752 to 131071, as said below
- query_up_weight: bfloat16 [1536, 12288], P('seq', 'head'), may hold values from -0.15625 to 0.15625
- adapter_down_factor: bfloat16 [3072, 64], P(('groups', 'seq')), parts along dimension 0, may hold values from -0.75 to 0.75
- adapter_up_factor: bfloat16 [128, 12288], P('groups', 'head'), parts along dimension 0, may hold values from -0.15625 to 0.15625
- head_key_up_weight: bfloat16 [64, 128, 512], P('head'), may hold values from -0.5 to 0.5
- head_value_up_weight: bfloat16 [64, 512, 128], P('head'), may hold values from -0.25 to 0.25
- output_projection_weight: bfloat16 [8192, 7168], P('head', 'seq'), may hold values from -0.0625 to 0.0625
Outputs:
- merged_weight: bfloat16 [3072, 12288], P(('groups', 'seq'), 'head'), parts along dimension 0
- mixed: bfloat16 [640, 7168], P(('groups', 'head'), 'seq'), parts along dimension 0
There are 2 independent parts, one for each index of `groups`. A program takes and returns all parts, laid end to end along the dimension named above; an argument that names none is the same for every part. Nothing has to cross between parts.
Inputs may be any that keep to these rules, and one draw needn't show every extreme that they name: positions are distinct; each aligned block of 80 rows holds 80 consecutive positions in rising order, and the blocks together cover the last 320 positions of the prompt in an order drawn from the seed.
All inputs are finite; a program needn't handle non-finite values.
Results may differ from a plain program's by a relative error of at most 0.015.
The roundings to bfloat16 on the way count: a program that leaves them out, or rounds other values in their place, can miss the bound.
Values may be sent and summed in bfloat16 or wider, within the bound.
A program may use at most 64 MiB of HBM per device.

v0:
```python
import math
import jax
import jax.numpy as jnp
from jax import lax
from jax.sharding import PartitionSpec as P


def on_device(
    query_latent_rows,
    key_value_latents,
    positions,
    query_up_weight,
    adapter_down_factor,
    adapter_up_factor,
    head_key_up_weight,
    head_value_up_weight,
    output_projection_weight,
):
    merged_query_weight = (
        query_up_weight.astype(jnp.float32)
        + jnp.dot(adapter_down_factor, adapter_up_factor, preferred_element_type=jnp.float32)
    ).astype(jnp.bfloat16)
    tok_rows = query_latent_rows.shape[0]
    queries = jnp.dot(
        query_latent_rows,
        lax.all_gather(merged_query_weight, "seq", axis=0, tiled=True),
        preferred_element_type=jnp.float32,
    )
    heads_dev = head_key_up_weight.shape[0]
    nope_dim = head_key_up_weight.shape[1]
    kv_rank = head_key_up_weight.shape[2]
    lat_width = key_value_latents.shape[1]
    score_scale = 1.0 / math.sqrt(nope_dim + lat_width - kv_rank)
    queries = queries.astype(jnp.bfloat16).reshape(tok_rows, heads_dev, -1)
    absorbed = jnp.einsum(
        "thn,hnk->thk",
        queries[:, :, :nope_dim],
        head_key_up_weight,
        preferred_element_type=jnp.float32,
    ).astype(jnp.bfloat16)
    full_query = jnp.concatenate([absorbed, queries[:, :, nope_dim:]], axis=2).reshape(
        tok_rows * heads_dev, lat_width
    )
    query_pos = jnp.repeat(positions, heads_dev)
    q_count = tok_rows * heads_dev
    row_max = jnp.full((q_count,), -1e30, jnp.float32)
    key_rows = lax.all_gather(key_value_latents, "seq", axis=0, tiled=True)
    key_pos = lax.all_gather(positions, "seq", axis=0, tiled=True)
    visible = key_pos[None, :] <= query_pos[:, None]
    scores = (
        lax.dot_general(
            full_query, key_rows, (((1,), (1,)), ((), ())), preferred_element_type=jnp.float32
        )
        * score_scale
    )
    scores = jnp.where(visible, scores, jnp.float32(-1e30))
    new_max = jnp.maximum(row_max, jnp.max(scores, axis=1))
    weights = jnp.where(visible, jnp.exp(scores - new_max[:, None]), jnp.float32(0.0))
    row_sum = jnp.sum(weights, axis=1)
    running = jnp.dot(
        weights.astype(jnp.bfloat16), key_rows[:, :kv_rank], preferred_element_type=jnp.float32
    )
    row_max, row_sum, running = (new_max, row_sum, running)
    context_output = (
        (running / row_sum[:, None]).astype(jnp.bfloat16).reshape(tok_rows, heads_dev, kv_rank)
    )
    heads_out = (
        jnp.einsum(
            "euw,uwz->euz", context_output, head_value_up_weight, preferred_element_type=jnp.float32
        )
        .astype(jnp.bfloat16)
        .reshape(tok_rows, -1)
    )
    partial_value = jnp.dot(
        lax.all_gather(heads_out, "seq", axis=0, tiled=True),
        output_projection_weight,
        preferred_element_type=jnp.float32,
    )
    mixed = lax.psum_scatter(
        partial_value.astype(jnp.bfloat16), "head", scatter_dimension=0, tiled=True
    )
    return (merged_query_weight, mixed)


def solution(mesh):
    placed = (
        P(("groups", "seq"), None),
        P(("groups", "seq"), None),
        P(("groups", "seq")),
        P("seq", "head"),
        P(("groups", "seq"), None),
        P("groups", "head"),
        P("head", None, None),
        P("head", None, None),
        P("head", "seq"),
    )
    return jax.shard_map(
        on_device,
        mesh=mesh,
        in_specs=placed,
        out_specs=(P(("groups", "seq"), "head"), P(("groups", "head"), "seq")),
        check_vma=False,
    )
```

profile of v0, /device:TPU:0, one launch (start us, length us, event | category | flops | bytes accessed | tf_op | source)
XLA Modules:
  0.0 269.0 jit_solution(17031424686050613375)
XLA Ops:
  7.2 0.0 all-gather.3.cloned.1.call-start
  7.2 4.2 %add_convert_fusion = bf16[384,3072]{1,0:T(8,128)(2,1)} fusion(bf16[384,3072]{1,0:T(8,128)(2,1)} %param.12, bf16[384,64]{0,1:T(8,128)(2,1)} %param.13, bf16[64,3072]{1,0:T(8,128)(2,1)} %param.14), kind=kOutput, calls=%fused_computation | convolution fusion | flops 154533888 | bytes 5160960 | tf_op jit(solution)/shard_map/dot_general | solution.py:21
  11.4 0.0 all-gather.3.cloned.1.call-update
  11.4 0.0 all-gather.5.cloned.1.call-start
  11.5 0.6 copy-done.5
  12.0 0.1 broadcast_in_dim.16
  12.1 0.1 le.16
  12.2 0.6 dynamic-slice
  13.4 0.2 dynamic-update-slice
  13.7 9.9 %all-reduce = s32[320]{0:T(512)S(1)} all-reduce(s32[320]{0:T(512)S(1)} %dynamic-update-slice), channel_id=1, replica_groups=mesh['groups'=2,'seq'=4,'head'=4] {'seq'}, use_global_device_ids=true, to_apply=%add | all-reduce | flops 320 | bytes 2560
  23.6 25.1 %all_gather.14 = bf16[320,576]{1,0:T(8,128)(2,1)} all-gather(bf16[80,576]{1,0:T(8,128)(2,1)S(1)} %copy-done.4), channel_id=1, replica_groups=mesh['groups'=2,'seq'=4,'head'=4] {'seq'}, dimensions={0}, use_global_device_ids=true | all-gather | bytes 460800 | tf_op jit(solution)/shard_map/all_gather | solution.py:47
  48.7 137.6 %all-gather.3.cloned.1.call-done = bf16[1536,3072]{1,0:T(8,128)(2,1)} async-done(((bf16[384,3072]{1,0:T(8,128)(2,1)}), bf16[1536,3072]{1,0:T(8,128)(2,1)}) %all-gather.3.cloned.1.call-update) | async-done | bytes 9437200 | tf_op jit(solution)/shard_map/all_gather | solution.py:26
  186.3 5.4 %fusion = bf16[80,3072]{1,0:T(8,128)(2,1)S(1)} fusion(bf16[80,1536]{1,0:T(8,128)(2,1)S(1)} %copy-done.2, bf16[1536,3072]{1,0:T(8,128)(2,1)} %all-gather.3.cloned.1.call-done), kind=kOutput, calls=%fused_computation.2 | convolution fusion | flops 755220480 | bytes 10174464 | tf_op jit(solution)/shard_map/dot_general | solution.py:24
  191.8 0.7 reshape.22
  192.5 0.1 slice.12
  192.6 0.1 slice.13
  192.6 0.1 copy.20
  192.7 0.5 fusion.3
  193.2 0.1 pad_maximum_fusion
  193.4 0.3 copy.16
  193.7 0.7 copy-done.3
  194.4 0.9 fusion.22
  195.3 0.3 fusion.6
  195.6 1.0 fusion.1
  196.6 0.6 copy-done.1
  197.2 1.6 fusion.11
  198.8 0.8 copy.31
  199.6 0.0 all-gather.5.cloned.1.call-update
  199.7 0.0 reduce-scatter.2.cloned.1.call-start
  199.7 31.0 %all-gather.5.cloned.1.call-done = bf16[320,2048]{1,0:T(8,128)(2,1)} async-done(((bf16[80,2048]{1,0:T(8,128)(2,1)}), bf16[320,2048]{1,0:T(8,128)(2,1)}) %all-gather.5.cloned.1.call-update) | async-done | bytes 1310736 | tf_op jit(solution)/shard_map/all_gather | solution.py:75
  230.7 7.0 %convolution_convert_fusion.1 = bf16[320,1792]{1,0:T(8,128)(2,1)} fusion(bf16[320,2048]{1,0:T(8,128)(2,1)} %all-gather.5.cloned.1.call-done, bf16[2048,1792]{1,0:T(8,128)(2,1)} %param.17), kind=kOutput, calls=%fused_computation.7 | convolution fusion | flops 2349383680 | bytes 9797632 | tf_op jit(solution)/shard_map/dot_general | solution.py:74
  237.8 24.7 %reduce-scatter.2.cloned.1.call-done = bf16[80,1792]{1,0:T(8,128)(2,1)} async-done(((bf16[320,1792]{1,0:T(8,128)(2,1)}), bf16[80,1792]{1,0:T(8,128)(2,1)}) %reduce-scatter.2.cloned.1.call-update) | async-done | bytes 286736 | tf_op jit(solution)/shard_map/reduce_scatter | solution.py:79
  (14 shorter events, 0.1 us)
Async XLA Ops:
  7.2 185.6 %copy-start = (bf16[16,128,512]{2,1,0:T(8,128)(2,1)S(1)}, bf16[16,128,512]{2,1,0:T(8,128)(2,1)}, u32[]{:S(2)}) copy-start(bf16[16,128,512]{2,1,0:T(8,128)(2,1)} %param.15) | copy-start | bytes 6291460
  7.2 179.2 %all-gather.3.cloned.1.call-start = ((), (), s32[]{:S(2)}) async-start(), calls=%async_computation.1 | async-start | bytes 11796480 | tf_op jit(solution)/shard_map/all_gather | solution.py:26
  11.4 0.7 copy-start.5
  11.4 0.8 copy-start.6
  11.4 12.2 %copy-start.4 = (bf16[80,576]{1,0:T(8,128)(2,1)S(1)}, bf16[80,576]{1,0:T(8,128)(2,1)}, u32[]{:S(2)}) copy-start(bf16[80,576]{1,0:T(8,128)(2,1)} %param.10) | copy-start | bytes 276484
  11.4 175.0 %copy-start.2 = (bf16[80,1536]{1,0:T(8,128)(2,1)S(1)}, bf16[80,1536]{1,0:T(8,128)(2,1)}, u32[]{:S(2)}) copy-start(bf16[80,1536]{1,0:T(8,128)(2,1)} %param.9) | copy-start | bytes 737284
  11.4 219.3 %all-gather.5.cloned.1.call-start = ((), (), s32[]{:S(2)}) async-start(), calls=%async_computation.2 | async-start | bytes 1638400 | tf_op jit(solution)/shard_map/all_gather | solution.py:75
  193.4 1.0 copy-start.3
  195.6 1.6 copy-start.1
  199.7 62.8 %reduce-scatter.2.cloned.1.call-start = ((), (), s32[]{:S(2)}) async-start(), calls=%async_computation.3 | async-start | bytes 1433600 | tf_op jit(solution)/shard_map/reduce_scatter | solution.py:79
Sparse Core Ops, SparseCore 0:
  11.5 174.7 all-gather.2
  199.8 30.8 all-gather.4
  237.9 24.5 reduce-scatter.1
where the time goes:
time: 269 us
  waiting for transfers between devices  193 us (72%)
  blocking collectives  35 us (13%)
  matrix products  20.6 us (8%)
  between operations  14.5 us (5%)
  local copies, waits for them, and re-layouts  4.87 us (2%)
    all_gather x1, waiting for transfers between devices, on_device(): lax.all_gather(merged_query_weight, 'seq', axis=0, tiled=True)  138 us
    all_gather x1, waiting for transfers between devices, on_device(): lax.all_gather(heads_out, 'seq', axis=0, tiled=True)  31 us
    all_gather x1, blocking collectives, on_device(): key_rows = lax.all_gather(key_value_latents, 'seq', axis=0, tiled=True)  25.1 us
    reduce_scatter x1, waiting for transfers between devices, on_device(): lax.psum_scatter(partial_value.astype(jnp.bfloat16), 'head', scatter_dime...  24.7 us
    unnamed x1, blocking collectives  9.92 us
    dot_general x1, matrix products, on_device(): jnp.dot(lax.all_gather(heads_out, 'seq', axis=0, tiled=True), output_proj...  7.02 us
    dot_general x1, matrix products, on_device(): jnp.dot(query_latent_rows, lax.all_gather(merged_query_weight, 'seq', axi...  5.42 us
  transfers between devices with their start and end apart: 3, of which 3 were waited for; matrix products, arithmetic and copies ran while one was open for 0% of the time, Pallas kernels for 0%

commit v1 on v0

--- a/solution.py
+++ b/solution.py
@@ -16,15 +16,20 @@
     head_value_up_weight,
     output_projection_weight,
 ):
+
+    def _close_islands(v0):
+        b_next = jax.lax.axis_size("seq")
+        state_next = jnp.stack(b_next * [v0], axis=0)
+        carry_out = jax.lax.all_to_all(state_next, axis_name="seq", split_axis=0, concat_axis=0)
+        return jnp.concatenate(carry_out, axis=0)
+
     merged_query_weight = (
         query_up_weight.astype(jnp.float32)
         + jnp.dot(adapter_down_factor, adapter_up_factor, preferred_element_type=jnp.float32)
     ).astype(jnp.bfloat16)
     tok_rows = query_latent_rows.shape[0]
     queries = jnp.dot(
-        query_latent_rows,
-        lax.all_gather(merged_query_weight, "seq", axis=0, tiled=True),
-        preferred_element_type=jnp.float32,
+        query_latent_rows, _close_islands(merged_query_weight), preferred_element_type=jnp.float32
     )
     heads_dev = head_key_up_weight.shape[0]
     nope_dim = head_key_up_weight.shape[1]

time: 269 us -> 329 us (1.22)
  blocking collectives: 35 us -> 221 us
  waiting for transfers between devices: 193 us -> 56 us
  starting transfers between devices: 0.12 us -> 6.54 us
  local copies, waits for them, and re-layouts: 4.87 us -> 10.7 us
    unnamed x1, blocking collectives: 9.92 us -> 205 us
    all_gather x1 -> x0, waiting for transfers between devices: 138 us -> none  [on_device(): lax.all_gather(merged_query_weight, 'seq', axis=0, tiled=True)]
    all_gather x1, blocking collectives: 25.1 us -> 15.8 us  [on_device(): key_rows = lax.all_gather(key_value_latents, 'seq', axis=0, tiled=True)]
    all_to_all x0 -> x1, starting transfers between devices: none -> 6.49 us  [_close_islands(): jax.lax.all_to_all(state_next, axis_name='seq', split_axis=0, concat_axis=0)]
    another operation x0 -> x1, local copies, waits for them, and re-layouts: none -> 5.01 us  [_close_islands(): state_next = jnp.stack(b_next * [v0], axis=0)]
  transfers between devices with their start and end apart: 3 -> 3, of which waited for: 3 -> 2; matrix products, arithmetic and copies ran while one was open for 0% -> 0% of each run, Pallas kernels for 0% -> 0%
where the time goes in v1:
time: 329 us
  blocking collectives  221 us (67%)
  waiting for transfers between devices  56 us (17%)
  matrix products  19.3 us (6%)
  between operations  14.8 us (4%)
  local copies, waits for them, and re-layouts  10.7 us (3%)
  starting transfers between devices  6.54 us (2%)
    unnamed x1, blocking collectives  205 us
    all_gather x1, waiting for transfers between devices, on_device(): lax.all_gather(heads_out, 'seq', axis=0, tiled=True)  31.3 us
    reduce_scatter x1, waiting for transfers between devices, on_device(): lax.psum_scatter(partial_value.astype(jnp.bfloat16), 'head', scatter_dime...  24.7 us
    all_gather x1, blocking collectives, on_device(): key_rows = lax.all_gather(key_value_latents, 'seq', axis=0, tiled=True)  15.8 us
    dot_general x1, matrix products, on_device(): jnp.dot(lax.all_gather(heads_out, 'seq', axis=0, tiled=True), output_proj...  7.02 us
  transfers between devices with their start and end apart: 3, of which 2 were waited for; matrix products, arithmetic and copies ran while one was open for 0% of the time, Pallas kernels for 0%

profile of v1, /device:TPU:0, one launch (start us, length us, event | category | flops | bytes accessed | tf_op | source)
XLA Modules:
  0.0 329.0 jit_solution(2136262747963615322)
XLA Ops:
  7.2 0.0 copy-start
  7.2 2.7 add_convert_fusion
  9.9 1.4 copy-done.1
  11.3 5.0 %stack.2 = bf16[4,384,3072]{2,1,0:T(8,128)(2,1)} broadcast(bf16[384,3072]{1,0:T(8,128)(2,1)S(1)} %add_convert_fusion), dimensions={1,2} | broadcast | bytes 11796480 | tf_op jit(solution)/shard_map/stack | solution.py:22
  16.4 6.5 %all-to-all-start = ((bf16[4,384,3072]{2,1,0:T(8,128)(2,1)}), bf16[4,384,3072]{2,1,0:T(8,128)(2,1)}, u32[]{:S(2)}, u32[]{:S(2)}) async-start(bf16[4,384,3072]{2,1,0:T(8,128)(2,1)} %stack.2), calls=%async_computation | async-start | bytes 18874368 | tf_op jit(solution)/shard_map/all_to_all | solution.py:23
  22.9 0.1 broadcast_in_dim.16
  22.9 0.1 le.16
  23.0 0.6 dynamic-slice
  24.3 0.2 dynamic-update-slice
  24.5 205.2 %all-reduce = s32[320]{0:T(512)S(1)} all-reduce(s32[320]{0:T(512)S(1)} %dynamic-update-slice), channel_id=1, replica_groups=mesh['groups'=2,'seq'=4,'head'=4] {'seq'}, use_global_device_ids=true, to_apply=%add | all-reduce | flops 320 | bytes 2560
  229.7 15.8 %all_gather.10 = bf16[320,576]{1,0:T(8,128)(2,1)} all-gather(bf16[80,576]{1,0:T(8,128)(2,1)S(1)} %copy-done.5), channel_id=1, replica_groups=mesh['groups'=2,'seq'=4,'head'=4] {'seq'}, dimensions={0}, use_global_device_ids=true | all-gather | bytes 460800 | tf_op jit(solution)/shard_map/all_gather | solution.py:52
  245.6 5.4 %fusion = bf16[80,3072]{1,0:T(8,128)(2,1)S(1)} fusion(bf16[80,1536]{1,0:T(8,128)(2,1)S(1)} %copy-done.3, bf16[1536,3072]{1,0:T(8,128)(2,1)} %bitcast.1), kind=kOutput, calls=%fused_computation.2 | convolution fusion | flops 755220480 | bytes 10174464 | tf_op jit(solution)/shard_map/dot_general | solution.py:31
  251.0 0.7 reshape.28
  251.8 0.1 slice.12
  251.8 0.1 slice.13
  251.9 0.1 copy.20
  252.0 0.5 fusion.3
  252.5 0.1 pad_maximum_fusion
  252.7 0.3 copy.16
  253.0 0.7 copy-done.4
  253.7 0.9 fusion.22
  254.5 0.3 fusion.6
  254.9 1.0 fusion.1
  255.9 0.6 copy-done.2
  256.5 1.7 fusion.11
  258.2 0.8 copy.31
  259.0 0.0 all-gather.2.cloned.1.call-update
  259.0 0.0 reduce-scatter.2.cloned.1.call-start
  259.1 31.3 %all-gather.2.cloned.1.call-done = bf16[320,2048]{1,0:T(8,128)(2,1)} async-done(((bf16[80,2048]{1,0:T(8,128)(2,1)}), bf16[320,2048]{1,0:T(8,128)(2,1)}) %all-gather.2.cloned.1.call-update) | async-done | bytes 1310736 | tf_op jit(solution)/shard_map/all_gather | solution.py:80
  290.4 7.0 %convolution_convert_fusion.1 = bf16[320,1792]{1,0:T(8,128)(2,1)} fusion(bf16[320,2048]{1,0:T(8,128)(2,1)} %all-gather.2.cloned.1.call-done, bf16[2048,1792]{1,0:T(8,128)(2,1)} %param.17), kind=kOutput, calls=%fused_computation.7 | convolution fusion | flops 2349383680 | bytes 9797632 | tf_op jit(solution)/shard_map/dot_general | solution.py:79
  297.4 0.0 reduce-scatter.2.cloned.1.call-update
  297.5 24.7 %reduce-scatter.2.cloned.1.call-done = bf16[80,1792]{1,0:T(8,128)(2,1)} async-done(((bf16[320,1792]{1,0:T(8,128)(2,1)}), bf16[80,1792]{1,0:T(8,128)(2,1)}) %reduce-scatter.2.cloned.1.call-update) | async-done | bytes 286736 | tf_op jit(solution)/shard_map/reduce_scatter | solution.py:84
  (16 shorter events, 0.0 us)
Async XLA Ops:
  7.2 244.8 %copy-start = (bf16[16,128,512]{2,1,0:T(8,128)(2,1)S(1)}, bf16[16,128,512]{2,1,0:T(8,128)(2,1)}, u32[]{:S(2)}) copy-start(bf16[16,128,512]{2,1,0:T(8,128)(2,1)} %param.15) | copy-start | bytes 6291460
  9.9 1.4 copy-start.1
  16.3 6.5 %copy-start.6 = (s32[80]{0:T(128)S(1)}, s32[80]{0:T(128)}, u32[]{:S(2)}) copy-start(s32[80]{0:T(128)} %param.11) | copy-start | bytes 964
  16.3 6.7 %copy-start.7 = (u32[32]{0:T(128)S(1)}, u32[32]{0:T(128)}, u32[]{:S(2)}) copy-start(u32[32]{0:T(128)} %constant.11) | copy-start | bytes 388
  16.3 213.4 %copy-start.5 = (bf16[80,576]{1,0:T(8,128)(2,1)S(1)}, bf16[80,576]{1,0:T(8,128)(2,1)}, u32[]{:S(2)}) copy-start(bf16[80,576]{1,0:T(8,128)(2,1)} %param.10) | copy-start | bytes 276484
  16.4 229.3 %copy-start.3 = (bf16[80,1536]{1,0:T(8,128)(2,1)S(1)}, bf16[80,1536]{1,0:T(8,128)(2,1)}, u32[]{:S(2)}) copy-start(bf16[80,1536]{1,0:T(8,128)(2,1)} %param.9) | copy-start | bytes 737284
  16.4 229.2 %all-to-all-start = ((bf16[4,384,3072]{2,1,0:T(8,128)(2,1)}), bf16[4,384,3072]{2,1,0:T(8,128)(2,1)}, u32[]{:S(2)}, u32[]{:S(2)}) async-start(bf16[4,384,3072]{2,1,0:T(8,128)(2,1)} %stack.2), calls=%async_computation | async-start | bytes 18874368 | tf_op jit(solution)/shard_map/all_to_all | solution.py:23
  22.8 267.6 %all-gather.2.cloned.1.call-start = ((), (), s32[]{:S(2)}) async-start(), calls=%async_computation.2 | async-start | bytes 1638400 | tf_op jit(solution)/shard_map/all_gather | solution.py:80
  252.7 1.0 copy-start.4
  254.9 1.6 copy-start.2
  259.0 63.1 %reduce-scatter.2.cloned.1.call-start = ((), (), s32[]{:S(2)}) async-start(), calls=%async_computation.3 | async-start | bytes 1433600 | tf_op jit(solution)/shard_map/reduce_scatter | solution.py:84
Sparse Core Ops, SparseCore 0:
  259.2 31.2 all-gather.1
  297.6 24.5 reduce-scatter.1
